TPU v7x, 32 devices: a whole 2x2x4 slice. The times are simulated.
32 devices in a mesh: col: 16 (over z, x, core), row: 2 (over y).
Axes of the slice: x: 2, y: 2, z: 4, core: 2. Of those that a mesh axis runs over, the one named last changes fastest.
Arguments:
- uniq_rows: bfloat16 [32, 128, 1536], P('row', 'col'), may hold values from -6 to 6
- row_ids: int32 [32, 128, 8], P('row', 'col'), may hold values from 0 to 255, as said below
- sample_idx: int32 [512, 128], P('row', 'col'), may hold values from 0 to 7, as said below
- fm_proj: bfloat16 [128, 8], replicated, may hold values from -0.5 to 0.5
- ln_gain: float32 [1024], replicated, may hold values from 0.5 to 1.5
- w_up: bfloat16 [1024, 2048], P(None, 'row'), may hold values from -0.1875 to 0.1875
- w_down: bfloat16 [2048, 1536], P('row'), may hold values from -0.125 to 0.125
- w_lc: bfloat16 [8, 128], replicated, may hold values from -0.5 to 0.5
- w_res: bfloat16 [16, 128], replicated, may hold values from -0.5 to 0.5
- out_gain: float32 [192], replicated, may hold values from 0.5 to 1.5
- cotangent: bfloat16 [512, 3072], P(('row', 'col')), may hold values from -6 to 6
- moment1: float32 [128, 256, 192], P('col', 'row'), may hold values from -1.5 to 1.5
- moment2: float32 [128, 256], P('col', 'row'), may hold values from 0.01 to 0.1
Outputs:
- layer_out: bfloat16 [512, 3072], P(('row', 'col'))
- new_moment1: float32 [128, 256, 192], P('col', 'row')
- new_moment2: float32 [128, 256], P('col', 'row')
- row_step: float32 [128, 256, 192], P('col', 'row')
Inputs may be any that keep to these rules, and one draw needn't show every extreme that they name: `sample_idx`: for each block of 16 samples and each slot, every one of the 8 list entries is used by at least one sample of the block. `row_ids`: the 8 ids of one list are distinct. Row v of a slot is owned by index v // 128 of row. Of the 1024 list entries held by one device (the blocks of its index of row, the slots of its index of col), at most 640 name rows of one owner, and in every draw some owner is named exactly 640 times on each device.
All inputs are finite; a program needn't handle non-finite values.
Results may differ from a plain program's by a relative error of at most 0.005.
Values may be sent and summed in bfloat16 or wider, within the bound.
A program may use at most 64 MiB of HBM per device.

v0:
```python
import jax
import jax.numpy as jnp
from jax import lax
from jax.sharding import PartitionSpec as P

HIGH = lax.Precision.HIGHEST


def layer_norm(values, gain):
    centered = values - jnp.mean(values, -1, keepdims=True)
    inverse = lax.rsqrt(jnp.mean(centered * centered, -1, keepdims=True) + 1e-05)
    normed = centered * inverse
    return (normed * gain, normed, inverse)


def norm_back(grad_out, normed, inverse):
    first = jnp.mean(grad_out, -1, keepdims=True)
    second = jnp.mean(grad_out * normed, -1, keepdims=True)
    return (grad_out - first - normed * second) * inverse


def silu_grad(values):
    sigma = jax.nn.sigmoid(values)
    return sigma * (1.0 + values * (1.0 - sigma))


def body(
    uniq_rows,
    row_ids,
    sample_idx,
    fm_proj,
    ln_gain,
    w_up,
    w_down,
    w_lc,
    w_res,
    out_gain,
    cotangent,
    moment1,
    moment2,
):
    columns = lax.axis_size("col")
    owners = lax.axis_size("row")
    slot_dev = uniq_rows.shape[1]
    width = out_gain.shape[0]
    uniq = uniq_rows.shape[2] // width
    samples = cotangent.shape[0]
    slots = slot_dev * columns
    vocab_dev = moment2.shape[1]
    rank = fm_proj.shape[1]
    fm_rows = w_down.shape[1] // width
    out_rows = w_res.shape[0]
    entry_iota = jnp.arange(uniq, dtype=jnp.int32)
    index_local = sample_idx.reshape(columns, samples, slot_dev)
    index = lax.all_to_all(index_local, "col", split_axis=0, concat_axis=2, tiled=True).reshape(
        samples, slots
    )
    picker = (index[:, :, None] == entry_iota).astype(jnp.bfloat16)
    moved = lax.all_to_all(uniq_rows, "col", split_axis=0, concat_axis=1, tiled=True)
    table = moved.reshape(slots, uniq, width)
    embed = jnp.einsum("stl,tle->ste", picker, table, preferred_element_type=jnp.float32).astype(
        jnp.bfloat16
    )
    compress = jnp.einsum("ste,tk->sek", embed, fm_proj, preferred_element_type=jnp.float32).astype(
        jnp.bfloat16
    )
    gram = jnp.einsum("ste,sek->stk", embed, compress, preferred_element_type=jnp.float32)
    flat = gram.reshape(samples, slots * rank)
    scaled, normed_in, inverse_in = layer_norm(flat, ln_gain)
    normal_in = scaled.astype(jnp.bfloat16)
    hidden_pre = jnp.dot(
        lax.all_gather(normal_in, "row", axis=0, tiled=True),
        w_up,
        preferred_element_type=jnp.float32,
    )
    hidden = jax.nn.silu(hidden_pre).astype(jnp.bfloat16)
    part_rows = hidden
    fm_out = lax.psum_scatter(
        jnp.dot(part_rows, w_down, preferred_element_type=jnp.float32),
        "row",
        scatter_dimension=0,
        tiled=True,
    )
    linear = jnp.einsum("lt,ste->sle", w_lc, embed, preferred_element_type=jnp.float32)
    joined = jnp.concatenate([fm_out.reshape(samples, fm_rows, width), linear], 1)
    normed_out, normed_rows, inverse_rows = layer_norm(joined, out_gain)
    residual = jnp.einsum("ot,ste->soe", w_res, embed, preferred_element_type=jnp.float32)
    layer_out = (normed_out + residual).reshape(samples, out_rows * width).astype(jnp.bfloat16)
    upstream = cotangent.astype(jnp.float32).reshape(samples, out_rows, width)
    grad_joined = norm_back(upstream * out_gain, normed_rows, inverse_rows)
    grad_fm = grad_joined[:, :fm_rows].reshape(samples, fm_rows * width).astype(jnp.bfloat16)
    grad_hidden = lax.dot_general(
        lax.all_gather(grad_fm, "row", axis=0, tiled=True),
        w_down,
        (((1,), (1,)), ((), ())),
        preferred_element_type=jnp.float32,
    )
    grad_pre = (grad_hidden * silu_grad(hidden_pre)).astype(jnp.bfloat16)
    part_rows = grad_pre
    grad_flat = lax.psum_scatter(
        lax.dot_general(
            part_rows, w_up, (((1,), (1,)), ((), ())), preferred_element_type=jnp.float32
        ).astype(jnp.bfloat16),
        "row",
        scatter_dimension=0,
        tiled=True,
    ).astype(jnp.float32)
    grad_gram = norm_back(grad_flat * ln_gain, normed_in, inverse_in).reshape(samples, slots, rank)
    grad_embed = jnp.einsum("stk,sek->ste", grad_gram, compress.astype(jnp.float32), precision=HIGH)
    grad_comp = jnp.einsum(
        "ste,stk->sek", embed, grad_gram, precision=HIGH, preferred_element_type=jnp.float32
    )
    grad_embed = grad_embed + jnp.einsum(
        "tk,sek->ste", fm_proj.astype(jnp.float32), grad_comp, precision=HIGH
    )
    grad_embed = grad_embed + jnp.einsum(
        "lt,sle->ste", w_lc.astype(jnp.float32), grad_joined[:, fm_rows:], precision=HIGH
    )
    grad_embed = grad_embed + jnp.einsum(
        "ot,soe->ste", w_res.astype(jnp.float32), upstream, precision=HIGH
    )
    list_grads = jnp.einsum("stl,ste->tle", picker.astype(jnp.float32), grad_embed, precision=HIGH)
    returned = lax.all_to_all(
        list_grads.reshape(columns, slot_dev, uniq * width),
        "col",
        split_axis=0,
        concat_axis=0,
        tiled=True,
    )
    entry_grads = returned.reshape(columns * slot_dev * uniq, width)
    row_list = row_ids.reshape(-1)
    slot_of = jnp.broadcast_to(
        jnp.arange(slot_dev, dtype=jnp.int32)[None, :, None], row_ids.shape
    ).reshape(-1)
    owner = row_list // vocab_dev
    target = slot_of * vocab_dev + row_list % vocab_dev
    span = slot_dev * vocab_dev
    entries = row_list.shape[0]
    capacity = 5 * entries // (4 * owners)
    onehot = (owner[:, None] == jnp.arange(owners, dtype=jnp.int32)).astype(jnp.int32)
    before = jnp.cumsum(onehot, 0) - onehot
    place = jnp.sum(before * onehot, 1)
    target_slot = owner * capacity + place
    bucket = jnp.zeros((owners * capacity, width), jnp.float32).at[target_slot].set(entry_grads)
    labels = (
        jnp.full((owners * capacity,), -1.0, jnp.float32)
        .at[target_slot]
        .set(target.astype(jnp.float32))
    )
    got_rows, got_labels = (
        lax.all_to_all(
            bucket.reshape(owners, capacity, width), "row", split_axis=0, concat_axis=0, tiled=True
        ),
        lax.all_to_all(
            labels.reshape(owners, capacity), "row", split_axis=0, concat_axis=0, tiled=True
        ),
    )
    segment = jnp.where(got_labels >= 0.0, got_labels, float(span)).astype(jnp.int32).reshape(-1)
    summed = jax.ops.segment_sum(got_rows.reshape(-1, width), segment, num_segments=span + 1)[:span]
    row_grads = summed.reshape(slot_dev, vocab_dev, width)
    new_moment1 = 0.9 * moment1 + 0.1 * row_grads
    new_moment2 = 0.99 * moment2 + 0.01 * jnp.mean(row_grads * row_grads, -1)
    row_step = new_moment1 * lax.rsqrt(new_moment2)[..., None]
    return (layer_out, new_moment1, new_moment2, row_step)


def solution(mesh):
    return jax.shard_map(
        body,
        mesh=mesh,
        in_specs=(
            P("row", "col", None),
            P("row", "col", None),
            P("row", "col"),
            P(),
            P(),
            P(None, "row"),
            P("row", None),
            P(),
            P(),
            P(),
            P(("row", "col"), None),
            P("col", "row", None),
            P("col", "row"),
        ),
        out_specs=(
            P(("row", "col"), None),
            P("col", "row", None),
            P("col", "row"),
            P("col", "row", None),
        ),
        check_vma=False,
    )
```

profile of v0, /device:TPU:0, one launch (start us, length us, event | category | flops | bytes accessed | tf_op | source)
XLA Modules:
  0.0 203.6 jit_solution(17181912444277728995)
XLA Ops:
  7.2 0.9 reshape.259
  8.2 13.6 %all_to_all.46 = s32[16,1,128]{2,1,0:T(1,128)S(1)} all-to-all(s32[16,1,128]{2,1,0:T(1,128)S(1)} %reshape.316), channel_id=1, replica_groups=mesh['col'=16,'row'=2] {'col'}, dimensions={0} | all-to-all | bytes 16384 | tf_op jit(solution)/shard_map/all_to_all | solution.py:55
  21.9 3.6 %all-to-all-start.1 = ((bf16[16,8,1536]{2,1,0:T(8,128)(2,1)}), bf16[16,8,1536]{2,1,0:T(8,128)(2,1)S(1)}, u32[]{:S(2)}, u32[]{:S(2)}) async-start(bf16[16,8,1536]{2,1,0:T(8,128)(2,1)} %param.13), calls=%async_computation.1 | async-start | bytes 786432 | tf_op jit(solution)/shard_map/all_to_all | solution.py:59
  26.0 0.7 reduce.7
  26.7 0.7 reshape.317
  27.4 1.5 bitcast_bitcast_fusion.1
  28.8 8.7 %all-to-all-done.1 = bf16[16,8,1536]{2,1,0:T(8,128)(2,1)S(1)} async-done(((bf16[16,8,1536]{2,1,0:T(8,128)(2,1)}), bf16[16,8,1536]{2,1,0:T(8,128)(2,1)S(1)}, u32[]{:S(2)}, u32[]{:S(2)}) %all-to-all-start.1) | async-done | bytes 393248 | tf_op jit(solution)/shard_map/all_to_all | solution.py:59
  37.5 1.2 reshape.260
  38.8 2.6 %fusion = bf16[16,128,192]{2,0,1:T(8,128)(2,1)} fusion(bf16[128,8,192]{2,1,0:T(8,128)(2,1)} %reshape.260, s32[16,128]{0,1:T(8,128)} %bitcast_bitcast_fusion.1), kind=kOutput, calls=%fused_computation.7 | convolution fusion | flops 6701056 | bytes 1187840 | tf_op jit(solution)/shard_map/stl,tle->ste/dot_general | solution.py:61
  41.4 2.6 %copy.98 = bf16[16,128,192]{1,2,0:T(8,128)(2,1)} copy(bf16[16,128,192]{2,0,1:T(8,128)(2,1)} %fusion) | data formatting | bytes 1572864 | tf_op jit(solution)/shard_map/convert_element_type | solution.py:61
  44.0 1.6 convolution_convert_fusion.1
  45.6 0.7 copy-done.7
  46.3 1.5 fusion.47
  47.8 1.0 copy.99
  49.1 1.2 copy.100
  50.4 4.6 %all_gather.6 = bf16[32,1024]{1,0:T(8,128)(2,1)S(1)} all-gather(bf16[16,1024]{1,0:T(8,128)(2,1)S(1)} %multiply_convert_fusion.2), channel_id=1, replica_groups=mesh['col'=16,'row'=2] {'row'}, dimensions={0}, use_global_device_ids=true | all-gather | bytes 98304 | tf_op jit(solution)/shard_map/all_gather | solution.py:72
  55.0 2.1 %fusion.48 = f32[32,1024]{1,0:T(8,128)S(1)} fusion(bf16[32,1024]{1,0:T(8,128)(2,1)S(1)} %all_gather.6, bf16[1024,1024]{1,0:T(8,128)(2,1)} %param.18), kind=kOutput, calls=%fused_computation.114 | convolution fusion | flops 67108864 | bytes 2293760 | tf_op jit(solution)/shard_map/dot_general | solution.py:71
  57.1 0.6 copy-done.2
  57.7 1.3 fusion.19
  59.3 1.6 convolution_bitcast_fusion.1
  60.9 8.0 %reduce-scatter.3.cloned.1.call-done = f32[16,1536]{1,0:T(8,128)} async-done(((f32[32,1536]{1,0:T(8,128)}), f32[16,1536]{1,0:T(8,128)}) %reduce-scatter.3.cloned.1.call-update) | async-done | bytes 98320 | tf_op jit(solution)/shard_map/reduce_scatter | solution.py:78
  68.9 1.0 reshape.262
  70.2 0.9 fusion.9
  71.2 0.9 subtract_multiply_fusion
  72.1 0.7 copy-done.4
  72.8 0.6 slice.29
  73.4 1.6 convert_element_type.72
  75.0 5.1 %all_gather.7 = bf16[32,1536]{1,0:T(8,128)(2,1)} all-gather(bf16[16,1536]{1,0:T(8,128)(2,1)} %convert_element_type.72), channel_id=1, replica_groups=mesh['col'=16,'row'=2] {'row'}, dimensions={0}, use_global_device_ids=true | all-gather | bytes 147456 | tf_op jit(solution)/shard_map/all_gather | solution.py:93
  80.0 4.0 %convolution_convert_fusion.2 = bf16[32,1024]{1,0:T(8,128)(2,1)} fusion(bf16[1024,1024]{1,0:T(8,128)(2,1)} %param.18, bf16[32,1536]{1,0:T(8,128)(2,1)} %all_gather.7, bf16[1024,1536]{1,0:T(8,128)(2,1)S(1)} %copy-done, f32[32,1024]{1,0:T(8,128)} %copy-done.2), kind=kOutput, calls=%fused_computation.15 | convolution fusion | flops 168099840 | bytes 5537792 | tf_op jit(solution)/shard_map/dot_general | solution.py:101
  84.1 3.5 %fusion.12 = f32[16,192,128]{2,1,0:T(8,128)} fusion(f32[16,16,192]{2,1,0:T(8,128)} %copy-done.4, bf16[8,128]{1,0:T(8,128)(2,1)} %param.20), kind=kOutput, calls=%fused_computation.36 | convolution fusion | flops 37748736 | bytes 1705984 | tf_op jit(solution)/shard_map/lt,sle->ste/dot_general | solution.py:116
  87.6 7.5 %reduce-scatter.5.cloned.1.call-done = bf16[16,1024]{1,0:T(8,128)(2,1)} async-done(((bf16[32,1024]{1,0:T(8,128)(2,1)}), bf16[16,1024]{1,0:T(8,128)(2,1)}) %reduce-scatter.5.cloned.1.call-update) | async-done | bytes 32784 | tf_op jit(solution)/shard_map/reduce_scatter | solution.py:100
  95.1 1.0 fusion.20
  96.2 1.6 subtract_multiply_fusion.2
  97.7 1.8 copy.107
  99.6 1.8 copy.108
  101.4 2.4 %fusion.50 = f32[16,192,8]{1,2,0:T(8,128)S(1)} fusion(bf16[16,128,192]{1,2,0:T(8,128)(2,1)} %copy.98, f32[16,128,8]{1,2,0:T(8,128)} %copy.108), kind=kOutput, calls=%fused_computation.116 | convolution fusion | flops 37748736 | bytes 950272 | tf_op jit(solution)/shard_map/ste,stk->sek/dot_general | solution.py:110
  103.8 1.9 fusion.49
  105.7 1.4 fusion.41
  107.2 1.6 bitcast_add_fusion
  108.8 3.0 %copy.111 = f32[16,128,192]{2,0,1:T(8,128)} copy(f32[16,128,192]{1,2,0:T(8,128)} %bitcast_add_fusion) | data formatting | bytes 3145728 | tf_op jit(solution)/shard_map/add | solution.py:119
  111.8 3.5 %fusion.8 = f32[128,8,192]{2,1,0:T(8,128)} fusion(f32[16,128,192]{2,0,1:T(8,128)} %copy.111, s32[16,128]{0,1:T(8,128)S(1)} %copy-done.6), kind=kOutput, calls=%fused_computation.25 | convolution fusion | flops 37765120 | bytes 2367488 | tf_op jit(solution)/shard_map/stl,ste->tle/dot_general | solution.py:122
  115.3 2.4 %reshape.270 = f32[16,8,1536]{2,1,0:T(8,128)} reshape(f32[128,8,192]{2,1,0:T(8,128)} %fusion.8) | data formatting | bytes 1572864 | tf_op jit(solution)/shard_map/reshape | solution.py:124
  117.7 5.8 %all-to-all-start.3 = ((f32[16,8,1536]{2,1,0:T(8,128)}), f32[16,8,1536]{2,1,0:T(8,128)}, u32[]{:S(2)}, u32[]{:S(2)}) async-start(f32[16,8,1536]{2,1,0:T(8,128)} %reshape.270), calls=%async_computation.5 | async-start | bytes 1572864 | tf_op jit(solution)/shard_map/all_to_all | solution.py:123
  124.0 0.6 reduce-window.6
  125.2 4.3 %scatter_custom_fusion = f32[1280]{0:T(1024)S(1)} fusion(s32[1024]{0:T(1024)S(1)} %bitcast.112, f32[1024]{0:T(1024)S(1)} %get-tuple-element.34, f32[]{:T(128)} %constant.65.clone.1), kind=kCustom, calls=%fused_computation.91 | custom fusion | bytes 5124 | tf_op jit(solution)/shard_map/scatter | solution.py:148
  129.6 0.6 all_to_all.36
  130.2 12.1 %all-to-all-done.3 = f32[16,8,1536]{2,1,0:T(8,128)} async-done(((f32[16,8,1536]{2,1,0:T(8,128)}), f32[16,8,1536]{2,1,0:T(8,128)}, u32[]{:S(2)}, u32[]{:S(2)}) %all-to-all-start.3) | async-done | bytes 786464 | tf_op jit(solution)/shard_map/all_to_all | solution.py:123
  142.3 3.2 %all-to-all-start.2 = ((f32[2,1,640]{2,1,0:T(1,128)}), f32[2,1,640]{2,1,0:T(1,128)S(1)}, u32[]{:S(2)}, u32[]{:S(2)}) async-start(f32[2,1,640]{2,1,0:T(1,128)} %all_to_all.36), calls=%async_computation.3 | async-start | bytes 10240 | tf_op jit(solution)/shard_map/all_to_all | solution.py:154
  145.5 2.4 %reshape.286 = f32[1024,192]{1,0:T(8,128)} reshape(f32[16,8,1536]{2,1,0:T(8,128)} %all-to-all-done.3) | data formatting | bytes 1572864 | tf_op jit(solution)/shard_map/reshape | solution.py:130
  148.0 6.4 %scatter_custom_fusion.1 = f32[1280,192]{1,0:T(8,128)} fusion(s32[1024]{0:T(1024)S(1)} %bitcast.113, f32[1024,192]{1,0:T(8,128)} %reshape.286, f32[]{:T(128)} %constant.59.clone.1), kind=kCustom, calls=%fused_computation.20 | custom fusion | bytes 983552 | tf_op jit(solution)/shard_map/scatter | solution.py:144
  154.4 2.7 %copy.112 = f32[2,640,192]{1,2,0:T(8,128)} copy(f32[2,640,192]{2,1,0:T(8,128)} %bitcast.105) | data formatting | bytes 1966080 | tf_op jit(solution)/shard_map/reshape | solution.py:152
  157.0 4.4 %all-to-all-start.4 = ((f32[2,640,192]{1,2,0:T(8,128)}), f32[2,640,192]{1,2,0:T(8,128)}, u32[]{:S(2)}, u32[]{:S(2)}) async-start(f32[2,640,192]{1,2,0:T(8,128)} %copy.112), calls=%async_computation.6 | async-start | bytes 1966080 | tf_op jit(solution)/shard_map/all_to_all | solution.py:151
  161.5 0.6 fusion.28
  162.1 1.7 fusion.2
  163.7 0.8 convert_element_type.67
  164.6 10.7 %all-to-all-done.4 = f32[2,640,192]{1,2,0:T(8,128)} async-done(((f32[2,640,192]{1,2,0:T(8,128)}), f32[2,640,192]{1,2,0:T(8,128)}, u32[]{:S(2)}, u32[]{:S(2)}) %all-to-all-start.4) | async-done | bytes 983072 | tf_op jit(solution)/shard_map/all_to_all | solution.py:151
  175.2 2.7 %copy.118 = f32[2,640,192]{2,1,0:T(8,128)} copy(f32[2,640,192]{1,2,0:T(8,128)} %all-to-all-done.4) | data formatting | bytes 1966080 | tf_op jit(solution)/shard_map/reshape | solution.py:159
  177.9 9.5 %scatter_custom_fusion.2 = f32[1025,192]{1,0:T(8,128)} fusion(s32[1280]{0:T(1024)} %fusion.28, f32[1280,192]{1,0:T(8,128)} %bitcast.108, f32[]{:T(128)} %constant.59.clone.1), kind=kCustom, calls=%fused_computation.22 | custom fusion | flops 245760 | bytes 787712 | tf_op jit(solution)/shard_map/scatter-add | solution.py:159
  187.4 2.3 %slice.24 = f32[1024,192]{1,0:T(8,128)} slice(f32[1025,192]{1,0:T(8,128)} %scatter_custom_fusion.2), slice={[0:1024], [0:192]} | slice | bytes 1572864 | tf_op jit(solution)/shard_map/slice | solution.py:159
  189.7 2.4 %copy.120 = f32[1024,192]{0,1:T(8,128)} copy(f32[1024,192]{1,0:T(8,128)} %slice.24) | data formatting | bytes 1572864
  192.1 1.3 multiply_bitcast_fusion
  193.6 0.6 fusion.46
  194.7 1.0 copy.117
  195.8 1.0 copy.116
  (69 shorter events, 3.4 us)
Async XLA Ops:
  7.2 50.6 %copy-start = (bf16[1024,1536]{1,0:T(8,128)(2,1)S(1)}, bf16[1024,1536]{1,0:T(8,128)(2,1)}, u32[]{:S(2)}) copy-start(bf16[1024,1536]{1,0:T(8,128)(2,1)} %param.19) | copy-start | bytes 9437188
  21.9 15.7 %all-to-all-start.1 = ((bf16[16,8,1536]{2,1,0:T(8,128)(2,1)}), bf16[16,8,1536]{2,1,0:T(8,128)(2,1)S(1)}, u32[]{:S(2)}, u32[]{:S(2)}) async-start(bf16[16,8,1536]{2,1,0:T(8,128)(2,1)} %param.13), calls=%async_computation.1 | async-start | bytes 786432 | tf_op jit(solution)/shard_map/all_to_all | solution.py:59
  25.4 43.5 %reduce-scatter.3.cloned.1.call-start = ((), (), s32[]{:S(2)}) async-start(), calls=%async_computation.7 | async-start | bytes 294912 | tf_op jit(solution)/shard_map/reduce_scatter | solution.py:78
  38.8 5.2 %copy-start.13 = (bf16[128,8]{0,1:T(8,128)(2,1)S(1)}, bf16[128,8]{0,1:T(8,128)(2,1)}, u32[]{:S(2)}) copy-start(bf16[128,8]{0,1:T(8,128)(2,1)} %param.16) | copy-start | bytes 6148
  44.0 6.4 %copy-start.9 = (f32[1024]{0:T(1024)S(1)}, f32[1024]{0:T(1024)}, u32[]{:S(2)}) copy-start(f32[1024]{0:T(1024)} %param.17) | copy-start | bytes 12292
  45.6 0.7 copy-start.7
  47.8 7.2 %copy-start.15 = (f32[16]{0:T(128)}, f32[16]{0:T(128)S(1)}, u32[]{:S(2)}) copy-start(f32[16]{0:T(128)S(1)} %broadcast_multiply_fusion.6) | copy-start | bytes 196
  49.1 5.9 %copy-start.16 = (f32[16]{0:T(128)}, f32[16]{0:T(128)S(1)}, u32[]{:S(2)}) copy-start(f32[16]{0:T(128)S(1)} %add_rsqrt_fusion.1) | copy-start | bytes 196
  50.3 8.7 %copy-start.3 = (f32[16,1024]{1,0:T(8,128)}, f32[16,1024]{1,0:T(8,128)S(1)}, u32[]{:S(2)}) copy-start(f32[16,1024]{1,0:T(8,128)S(1)} %copy.100) | copy-start | bytes 196612
  57.1 0.6 copy-start.2
  57.7 1.4 copy-start.8
  57.7 1.6 copy-start.12
  59.0 36.0 %reduce-scatter.5.cloned.1.call-start = ((), (), s32[]{:S(2)}) async-start(), calls=%async_computation.8 | async-start | bytes 98304 | tf_op jit(solution)/shard_map/reduce_scatter | solution.py:100
  72.1 0.7 copy-start.4
  101.4 4.3 %copy-start.14 = (bf16[128,8]{0,1:T(8,128)(2,1)S(1)}, bf16[128,8]{0,1:T(8,128)(2,1)}, u32[]{:S(2)}) copy-start(bf16[128,8]{0,1:T(8,128)(2,1)} %param.16) | copy-start | bytes 6148
  103.8 3.3 %copy-start.1 = (f32[16,192,128]{2,1,0:T(8,128)S(1)}, f32[16,192,128]{2,1,0:T(8,128)}, u32[]{:S(2)}) copy-start(f32[16,192,128]{2,1,0:T(8,128)} %fusion.12) | copy-start | bytes 4718596
  103.8 3.3 %copy-start.11 = (bf16[16,128]{1,0:T(8,128)(2,1)S(1)}, bf16[16,128]{1,0:T(8,128)(2,1)}, u32[]{:S(2)}) copy-start(bf16[16,128]{1,0:T(8,128)(2,1)} %param.21) | copy-start | bytes 12292
  108.8 3.0 %copy-start.6 = (s32[16,128]{0,1:T(8,128)S(1)}, s32[16,128]{0,1:T(8,128)}, u32[]{:S(2)}) copy-start(s32[16,128]{0,1:T(8,128)} %bitcast_bitcast_fusion.1) | copy-start | bytes 24580
  115.3 8.3 %copy-start.10 = (s32[16,8,8]{0,2,1:T(8,128)S(1)}, s32[16,8,8]{0,2,1:T(8,128)}, u32[]{:S(2)}) copy-start(s32[16,8,8]{0,2,1:T(8,128)} %param.14) | copy-start | bytes 12292
  117.7 24.6 %all-to-all-start.3 = ((f32[16,8,1536]{2,1,0:T(8,128)}), f32[16,8,1536]{2,1,0:T(8,128)}, u32[]{:S(2)}, u32[]{:S(2)}) async-start(f32[16,8,1536]{2,1,0:T(8,128)} %reshape.270), calls=%async_computation.5 | async-start | bytes 1572864 | tf_op jit(solution)/shard_map/all_to_all | solution.py:123
  142.3 14.7 %all-to-all-start.2 = ((f32[2,1,640]{2,1,0:T(1,128)}), f32[2,1,640]{2,1,0:T(1,128)S(1)}, u32[]{:S(2)}, u32[]{:S(2)}) async-start(f32[2,1,640]{2,1,0:T(1,128)} %all_to_all.36), calls=%async_computation.3 | async-start | bytes 10240 | tf_op jit(solution)/shard_map/all_to_all | solution.py:154
  157.0 18.2 %all-to-all-start.4 = ((f32[2,640,192]{1,2,0:T(8,128)}), f32[2,640,192]{1,2,0:T(8,128)}, u32[]{:S(2)}, u32[]{:S(2)}) async-start(f32[2,640,192]{1,2,0:T(8,128)} %copy.112), calls=%async_computation.6 | async-start | bytes 1966080 | tf_op jit(solution)/shard_map/all_to_all | solution.py:151
  192.1 1.5 copy-start.17
  192.1 2.1 %copy-start.5 = (f32[8,128,192]{1,2,0:T(8,128)S(1)}, f32[8,128,192]{1,2,0:T(8,128)}, u32[]{:S(2)}) copy-start(f32[8,128,192]{1,2,0:T(8,128)} %param.24) | copy-start | bytes 2359300
Sparse Core Ops, SparseCore 0:
  59.2 9.7 reduce-scatter.2
  84.2 10.8 reduce-scatter.4
where the time goes:
time: 206 us; the launch traced here: 204 us
  local copies, waits for them, and re-layouts  51.8 us (25%)
  waiting for transfers between devices  47.1 us (23%)
  matrix products  30.7 us (15%)
  blocking collectives  23.3 us (11%)
  other arithmetic  19.3 us (9%)
  starting transfers between devices  17.1 us (8%)
  between operations  14.4 us (7%)
    all_to_all x1, blocking collectives, body(): lax.all_to_all(index_local, 'col', split_axis=0, concat_axis=2, tiled=True)  13.6 us
    all_to_all x1, waiting for transfers between devices, body(): lax.all_to_all(list_grads.reshape(columns, slot_dev, uniq * width), 'col'...  12.1 us
    all_to_all x1, waiting for transfers between devices, body(): lax.all_to_all(bucket.reshape(owners, capacity, width), 'row', split_axis...  10.7 us
    scatter-add x1, other arithmetic, body(): jax.ops.segment_sum(got_rows.reshape(-1, width), segment, num_segments=sp...  9.49 us
    all_to_all x1, waiting for transfers between devices, body(): lax.all_to_all(uniq_rows, 'col', split_axis=0, concat_axis=1, tiled=True)  8.72 us
    reduce_scatter x1, waiting for transfers between devices, body(): lax.psum_scatter(jnp.dot(part_rows, w_down, preferred_element_type=jnp.fl...  8 us
    unnamed x43, local copies, waits for them, and re-layouts  7.56 us
    reduce_scatter x1, waiting for transfers between devices, body(): lax.psum_scatter(lax.dot_general(part_rows, w_up, (((1,), (1,)), ((), ())...  7.52 us
  transfers between devices with their start and end apart: 6, of which 5 were waited for; matrix products, arithmetic and copies ran while one was open for 14% of the time, Pallas kernels for 0%

commit v1 on v0

--- a/solution.py
+++ b/solution.py
@@ -1,6 +1,10 @@
+import functools
+
 import jax
 import jax.numpy as jnp
 from jax import lax
+from jax.experimental import pallas as pl
+from jax.experimental.pallas import tpu as pltpu
 from jax.sharding import PartitionSpec as P
 
 HIGH = lax.Precision.HIGHEST
@@ -24,7 +28,7 @@
     return sigma * (1.0 + values * (1.0 - sigma))
 
 
-def body(
+def plain_body(
     uniq_rows,
     row_ids,
     sample_idx,
@@ -164,9 +168,517 @@
     return (layer_out, new_moment1, new_moment2, row_step)
 
 
+F32 = jnp.float32
+BF16 = jnp.bfloat16
+NT = (((1,), (1,)), ((), ()))
+
+
+def iota(shape, dim):
+    return lax.broadcasted_iota(jnp.int32, shape, dim)
+
+
+def matmul(a, b, dims=(((1,), (0,)), ((), ())), precision=None):
+    return lax.dot_general(a, b, dims, precision=precision, preferred_element_type=F32)
+
+
+def fused_kernel(
+    C,
+    R,
+    D,
+    uniq,
+    rid,
+    sidx,
+    fmp,
+    gain,
+    wup,
+    wdn,
+    wlc,
+    wres,
+    og,
+    cot,
+    lay_out,
+    rg_out,
+    land,
+    iland,
+    wraw,
+    wp,
+    wd,
+    t32,
+    tst,
+    lm,
+    lmask,
+    arep,
+    rmat,
+    nrm,
+    ggr,
+    nall,
+    y,
+    ds,
+    fown,
+    fsend,
+    frecv,
+    fm,
+    gall,
+    qown,
+    qsend,
+    qrecv,
+    lay32,
+    gf32,
+    lg,
+    sb,
+    rland,
+    oh,
+    enta,
+    entb,
+    owna,
+    psa,
+    pra,
+    psb,
+    prb,
+    loc,
+    s1,
+    r1,
+    si,
+    ri,
+    sa,
+    ra,
+    sbs,
+    rbs,
+    sx,
+    rx,
+):
+    S, E, U, K, T = 16, 192, 8, 8, 128
+    DV = D * T
+    me = lax.axis_index("col")
+    mr = lax.axis_index("row")
+
+    def to_col(i):
+        return lax.rem(me + i, C)
+
+    def from_col(i):
+        return lax.rem(me + C - i, C)
+
+    def to_row(i):
+        return lax.rem(mr + i, R)
+
+    def from_row(i):
+        return lax.rem(mr + R - i, R)
+
+    def rcopy(src, dst, ssem, rsem, where):
+        return pltpu.make_async_remote_copy(
+            src_ref=src,
+            dst_ref=dst,
+            send_sem=ssem,
+            recv_sem=rsem,
+            device_id=where,
+            device_id_type=pl.DeviceIdType.MESH,
+        )
+
+    cp_up = pltpu.make_async_copy(wup, wraw, loc.at[0])
+    cp_dn = pltpu.make_async_copy(wdn, wd, loc.at[1])
+    own_rows = pltpu.make_async_copy(uniq.at[me], land.at[me], loc.at[2])
+    own_idx = pltpu.make_async_copy(sidx.at[me], iland.at[me], loc.at[3])
+    cp_up.start()
+    cp_dn.start()
+    own_rows.start()
+    own_idx.start()
+
+    barrier = pltpu.get_barrier_semaphore()
+    for i in range(1, C):
+        pl.semaphore_signal(
+            barrier, inc=1, device_id={"col": to_col(i)}, device_id_type=pl.DeviceIdType.MESH
+        )
+    for i in range(1, R):
+        pl.semaphore_signal(
+            barrier, inc=1, device_id={"row": to_row(i)}, device_id_type=pl.DeviceIdType.MESH
+        )
+    pl.semaphore_wait(barrier, C + R - 2)
+
+    order = sorted(range(1, C), key=lambda i: -min(i, C - i))
+    idx_copies, row_copies = [], []
+    for i in order:
+        p = to_col(i)
+        idx_copies.append(rcopy(sidx.at[p], iland.at[me], si.at[i], ri.at[i], {"col": p}))
+        idx_copies[-1].start()
+    for i in order:
+        p = to_col(i)
+        row_copies.append(rcopy(uniq.at[p], land.at[me], s1.at[i], r1.at[i], {"col": p}))
+        row_copies[-1].start()
+
+    eye8 = (iota((K, K), 0) == iota((K, K), 1)).astype(F32)
+    pr, pc = iota((256, 256), 0), iota((256, 256), 1)
+    perm = (((pr & 31) * 8 + (pr >> 5)) == pc).astype(F32).astype(BF16)
+    cp_up.wait()
+    for g in range(4):
+        blk = matmul(perm, wraw[g * 256 : (g + 1) * 256, :]).astype(BF16)
+        for k in range(K):
+            wp[k * T + g * 32 : k * T + (g + 1) * 32, :] = blk[k * 32 : (k + 1) * 32, :]
+    lane = iota((K, K * T), 1)
+    spread = jnp.where((lane & 7) == iota((K, K * T), 0), gain[...], 0.0)
+    fold = ((iota((K * T, T), 0) >> 3) == iota((K * T, T), 1)).astype(F32)
+    gk = matmul(spread, fold, precision=HIGH)
+
+    amat = jnp.concatenate(
+        [
+            matmul(eye8.astype(BF16), fmp[...], NT),
+            wlc[...].astype(F32),
+            wres[...].astype(F32),
+        ],
+        0,
+    )
+    for j in range(32):
+        arep[j * S : (j + 1) * S, :] = jnp.broadcast_to(amat[j : j + 1, :], (S, T))
+
+    labels = matmul(eye8, rid[...].astype(F32).reshape(C * D, U), NT, HIGH).astype(jnp.int32)
+    slot_lane = iota((U, T), 1) & (D - 1)
+    target = iota((DV, T), 0)
+    for i in range(R):
+        local = labels - to_row(i) * T
+        key = jnp.where((local >= 0) & (local < T), slot_lane * T + local, -1)
+        for u in range(U):
+            oh[i, :, u * T : (u + 1) * T] = jnp.where(
+                target == jnp.broadcast_to(key[u : u + 1, :], (DV, T)), 1.0, 0.0
+            ).astype(BF16)
+
+    own_idx.wait()
+    for cp in idx_copies:
+        cp.wait_recv()
+    ix = iland[...].astype(F32).reshape(C * S, D)
+    tl = iota((C * S, T), 1)
+    placed = jnp.zeros((C * S, T), F32)
+    for d in range(D):
+        placed = jnp.where((tl & (D - 1)) == d, ix[:, d : d + 1], placed)
+    placed = jnp.where((tl >> (D.bit_length() - 1)) == (iota((C * S, T), 0) >> 4), placed, 0.0)
+    ist = jnp.sum(placed.reshape(C, S, T), 0)
+    idx_t = jnp.concatenate([ist] * 8, 0)
+    idx_n = idx_t.T
+    for u in range(U):
+        for q in range(4):
+            lm[q * T : (q + 1) * T, u * T : (u + 1) * T] = jnp.where(
+                idx_t == float(u), arep[q * T : (q + 1) * T, :], 0.0
+            ).astype(BF16)
+    for q in range(4):
+        turned = arep[q * T : (q + 1) * T, :].T
+        for u in range(U):
+            lmask[u * T : (u + 1) * T, q * T : (q + 1) * T] = jnp.where(
+                idx_n == float(u), turned, 0.0
+            ).astype(BF16)
+    upstream = cot[...].astype(F32)
+    for o in range(16):
+        rmat[(16 + o) * S : (17 + o) * S, :] = upstream[:, o * E : (o + 1) * E].astype(BF16)
+
+    own_rows.wait()
+    for cp in row_copies:
+        cp.wait_recv()
+    t32[...] = land[...].astype(F32).reshape(T, U * E)
+    for u in range(U):
+        tst[u * T : (u + 1) * T, :] = t32[:, u * E : (u + 1) * E].astype(BF16)
+
+    comp = matmul(lm[0:T, :], tst[...]).astype(BF16)
+    rmat[512:640, :] = comp
+    z = matmul(comp, tst[...], NT)
+    gram = jnp.where(idx_t == 0.0, z[:, 0:T], 0.0)
+    for u in range(1, U):
+        gram = gram + jnp.where(idx_t == float(u), z[:, u * T : (u + 1) * T], 0.0)
+    n_flat = float(K * T)
+    g3 = gram.reshape(K, S, T)
+    mu = jnp.sum(jnp.sum(g3, 0), -1, keepdims=True) / n_flat
+    cent = g3 - mu[None]
+    inv_in = lax.rsqrt(jnp.sum(jnp.sum(cent * cent, 0), -1, keepdims=True) / n_flat + 1e-05)
+    normed_in = cent * inv_in[None]
+    nrm[...] = normed_in.reshape(K * S, T)
+    for k in range(K):
+        nall[mr, :, k * T : (k + 1) * T] = (normed_in[k] * gk[k : k + 1, :]).astype(BF16)
+
+    def row_send(stage, src_of, dst):
+        copies = []
+        for i in range(1, R):
+            p = to_row(i)
+            sem = stage * R + i
+            copies.append(rcopy(src_of(p), dst.at[mr], sx.at[sem], rx.at[sem], {"row": p}))
+            copies[-1].start()
+        return copies
+
+    n_copies = row_send(0, lambda p: nall.at[mr], nall)
+    y[...] = matmul(lm[T:512, :], tst[...])
+    cp_dn.wait()
+    for cp in n_copies:
+        cp.wait_recv()
+    hp = matmul(nall[...].reshape(R * S, K * T), wp[...])
+    sg = jax.nn.sigmoid(hp)
+    hid = (hp * sg).astype(BF16)
+    fp = matmul(hid, wd[...]).reshape(R, S, 8 * E)
+    fsend[...] = fp.astype(BF16)
+    fown[...] = fp
+    f_copies = row_send(1, lambda p: fsend.at[p], frecv)
+    ds[...] = sg * (1.0 + hp * (1.0 - sg))
+
+    gain_out = og[...]
+
+    def out_norm(joined, o):
+        up = upstream[:, o * E : (o + 1) * E]
+        c = joined - jnp.mean(joined, -1, keepdims=True)
+        inv = lax.rsqrt(jnp.mean(c * c, -1, keepdims=True) + 1e-05)
+        nr = c * inv
+        return nr, norm_back(up * gain_out, nr, inv)
+
+    for o in range(8, 16):
+        nr, gj = out_norm(y[(o - 8) * S : (o - 7) * S, :], o)
+        lay32[:, o * E : (o + 1) * E] = nr * gain_out + y[(8 + o) * S : (9 + o) * S, :]
+        rmat[o * S : (o + 1) * S, :] = gj.astype(BF16)
+
+    for cp in f_copies:
+        cp.wait_recv()
+    total = fown[mr]
+    for i in range(1, R):
+        total = total + frecv[from_row(i)].astype(F32)
+    fm[...] = total
+    for o in range(8):
+        nr, gj = out_norm(fm[:, o * E : (o + 1) * E], o)
+        lay32[:, o * E : (o + 1) * E] = nr * gain_out + y[(8 + o) * S : (9 + o) * S, :]
+        gf32[:, o * E : (o + 1) * E] = gj
+    gall[mr] = gf32[...].astype(BF16)
+    g_copies = row_send(2, lambda p: gall.at[mr], gall)
+    lay_out[...] = lay32[...].astype(BF16)
+    for cp in g_copies:
+        cp.wait_recv()
+    gh = matmul(gall[...].reshape(R * S, 8 * E), wd[...], NT)
+    gp = (gh * ds[...]).astype(BF16)
+    gq = matmul(gp, wp[...], NT).reshape(R, S, K * T)
+    qsend[...] = gq.astype(BF16)
+    qown[...] = gq
+    q_copies = row_send(3, lambda p: qsend.at[p], qrecv)
+    for cp in q_copies:
+        cp.wait_recv()
+    gflat = qown[mr]
+    for i in range(1, R):
+        gflat = gflat + qrecv[from_row(i)].astype(F32)
+    qs = [gflat[:, k * T : (k + 1) * T] * gk[k : k + 1, :] for k in range(K)]
+    ns = [nrm[k * S : (k + 1) * S, :] for k in range(K)]
+    first = jnp.sum(sum(qs), -1, keepdims=True) / n_flat
+    second = jnp.sum(sum(q * n for q, n in zip(qs, ns)), -1, keepdims=True) / n_flat
+    for k in range(K):
+        ggr[k * S : (k + 1) * S, :] = (qs[k] - first - ns[k] * second) * inv_in
+    gg = ggr[...]
+    ggt = gg.T
+    for u in range(U):
+        lm[0:T, u * T : (u + 1) * T] = jnp.where(idx_t == float(u), gg, 0.0).astype(BF16)
+        lmask[u * T : (u + 1) * T, 512:640] = jnp.where(idx_n == float(u), ggt, 0.0).astype(BF16)
+    rmat[0:T, :] = matmul(lm[0:T, :], tst[...]).astype(BF16)
+    lg[...] = matmul(lmask[...], rmat[...])
+
+    half = iota((T, T), 1) < 64
+
+    def lo(u):
+        return lg[u * T : (u + 1) * T, 0:T].reshape(C, D, T)
+
+    def hi(u):
+        a = lg[u * T : (u + 1) * T, T:E]
+        b = lg[(u + 4) * T : (u + 5) * T, T:E]
+        return jnp.concatenate([a, b], 1).reshape(C, D, T)
+
+    for p in range(2):
+        sb[:, 64 + p * 16 : 80 + p * 16, :] = jnp.concatenate([hi(2 * p), hi(2 * p + 1)], 1).astype(
+            BF16
+        )
+    for p in range(4):
+        sb[:, p * 16 : (p + 1) * 16, :] = jnp.concatenate([lo(2 * p), lo(2 * p + 1)], 1).astype(
+            BF16
+        )
+    cut_a, cut_b = pl.ds(0, 64), pl.ds(64, 32)
+    b_copies, a_copies = [], []
+    for i in order:
+        p = to_col(i)
+        b_copies.append(
+            rcopy(sb.at[p, cut_b], rland.at[me, cut_b], sbs.at[i], rbs.at[i], {"col": p})
+        )
+        b_copies[-1].start()
+    for i in order:
+        p = to_col(i)
+        a_copies.append(rcopy(sb.at[p, cut_a], rland.at[me, cut_a], sa.at[i], ra.at[i], {"col": p}))
+        a_copies[-1].start()
+    rland[me] = sb[me]
+
+    for cp in b_copies:
+        cp.wait_recv()
+    for p in range(2):
+        both = rland[:, 64 + p * 16 : 80 + p * 16, :].astype(F32)
+        for h in range(2):
+            u = 2 * p + h
+            x = both[:, h * D : (h + 1) * D, :].reshape(T, T)
+            entb[u * T : (u + 1) * T, :] = x.astype(BF16)
+            entb[(u + 4) * T : (u + 5) * T, :] = pltpu.roll(x, 64, 1).astype(BF16)
+    hd = DV // 2
+    low = iota((hd, T), 1) < 64
+    p_copies = []
+    for i in range(1, R):
+        full = matmul(oh[i], entb[...])
+        psb[i] = jnp.where(low, full[:hd], pltpu.roll(full[hd:], 64, 1)).astype(BF16)
+        p_copies.append(
+            rcopy(psb.at[i], prb.at[i], sx.at[4 * R + i], rx.at[4 * R + i], {"row": to_row(i)})
+        )
+        p_copies[-1].start()
+    rg_out[:, T:E] = matmul(oh[0], entb[...])[:, : E - T]
+
+    for cp in a_copies:
+        cp.wait_recv()
+    for p in range(4):
+        both = rland[:, p * 16 : (p + 1) * 16, :].astype(F32)
+        for h in range(2):
+            u = 2 * p + h
+            enta[u * T : (u + 1) * T, :] = both[:, h * D : (h + 1) * D, :].reshape(T, T).astype(BF16)
+    for i in range(1, R):
+        psa[i] = matmul(oh[i], enta[...]).astype(BF16)
+        p_copies.append(
+            rcopy(psa.at[i], pra.at[i], sx.at[5 * R + i], rx.at[5 * R + i], {"row": to_row(i)})
+        )
+        p_copies[-1].start()
+    owna[...] = matmul(oh[0], enta[...])
+    for cp in p_copies:
+        cp.wait_recv()
+    total = owna[...]
+    for i in range(1, R):
+        total = total + pra[i].astype(F32)
+    rg_out[:, 0:T] = total
+    for i in range(1, R):
+        x = prb[i].astype(F32)
+        rg_out[:hd, T:E] += x[:, : E - T]
+        rg_out[hd:, T:E] += pltpu.roll(x, 64, 1)[:, : E - T]
+
+    for group in (
+        idx_copies,
+        row_copies,
+        n_copies,
+        f_copies,
+        g_copies,
+        q_copies,
+        b_copies,
+        a_copies,
+        p_copies,
+    ):
+        for cp in group:
+            cp.wait_send()
+
+
+def fast_body(
+    C,
+    R,
+    uniq_rows,
+    row_ids,
+    sample_idx,
+    fm_proj,
+    ln_gain,
+    w_up,
+    w_down,
+    w_lc,
+    w_res,
+    out_gain,
+    cotangent,
+    moment1,
+    moment2,
+):
+    D = uniq_rows.shape[1]
+    S = cotangent.shape[0]
+    hid = w_up.shape[1]
+    wide = w_down.shape[1]
+    flat = w_up.shape[0]
+    width = out_gain.shape[0]
+    T = C * D
+    DV = D * T
+    vmem = pl.BlockSpec(memory_space=pltpu.VMEM)
+    hbm = pl.BlockSpec(memory_space=pl.ANY)
+    dma = pltpu.SemaphoreType.DMA
+    layer_out, row_grads = pl.pallas_call(
+        functools.partial(fused_kernel, C, R, D),
+        out_shape=(
+            jax.ShapeDtypeStruct((S, 16 * width), BF16),
+            jax.ShapeDtypeStruct((DV, width), F32),
+        ),
+        in_specs=[hbm, vmem, hbm, vmem, vmem, hbm, hbm, vmem, vmem, vmem, vmem],
+        out_specs=(vmem, vmem),
+        scratch_shapes=[
+            pltpu.VMEM((C, D, wide), BF16),
+            pltpu.VMEM((C, S, D), jnp.int32),
+            pltpu.VMEM((flat, hid), BF16),
+            pltpu.VMEM((flat, hid), BF16),
+            pltpu.VMEM((hid, wide), BF16),
+            pltpu.VMEM((T, wide), F32),
+            pltpu.VMEM((8 * T, width), BF16),
+            pltpu.VMEM((512, 8 * T), BF16),
+            pltpu.VMEM((8 * T, 640), BF16),
+            pltpu.VMEM((512, T), F32),
+            pltpu.VMEM((640, width), BF16),
+            pltpu.VMEM((128, T), F32),
+            pltpu.VMEM((128, T), F32),
+            pltpu.VMEM((R, S, flat), BF16),
+            pltpu.VMEM((384, width), F32),
+            pltpu.VMEM((R * S, hid), F32),
+            pltpu.VMEM((R, S, wide), F32),
+            pltpu.VMEM((R, S, wide), BF16),
+            pltpu.VMEM((R, S, wide), BF16),
+            pltpu.VMEM((S, wide), F32),
+            pltpu.VMEM((R, S, wide), BF16),
+            pltpu.VMEM((R, S, flat), F32),
+            pltpu.VMEM((R, S, flat), BF16),
+            pltpu.VMEM((R, S, flat), BF16),
+            pltpu.VMEM((S, 16 * width), F32),
+            pltpu.VMEM((S, wide), F32),
+            pltpu.VMEM((8 * T, width), F32),
+            pltpu.VMEM((C, 12 * D, T), BF16),
+            pltpu.VMEM((C, 12 * D, T), BF16),
+            pltpu.VMEM((R, DV, 8 * T), BF16),
+            pltpu.VMEM((8 * T, T), BF16),
+            pltpu.VMEM((8 * T, T), BF16),
+            pltpu.VMEM((DV, T), F32),
+            pltpu.VMEM((R, DV, T), BF16),
+            pltpu.VMEM((R, DV, T), BF16),
+            pltpu.VMEM((R, DV // 2, T), BF16),
+            pltpu.VMEM((R, DV // 2, T), BF16),
+            dma((4,)),
+            dma((C,)),
+            dma((C,)),
+            dma((C,)),
+            dma((C,)),
+            dma((C,)),
+            dma((C,)),
+            dma((C,)),
+            dma((C,)),
+            dma((6 * R,)),
+            dma((6 * R,)),
+        ],
+        compiler_params=pltpu.CompilerParams(
+            collective_id=0, has_side_effects=True, vmem_limit_bytes=56 * 1024 * 1024
+        ),
+        name="wukong_step",
+    )(
+        uniq_rows,
+        row_ids,
+        sample_idx.reshape(C, S, D),
+        fm_proj,
+        ln_gain.reshape(1, flat),
+        w_up,
+        w_down,
+        w_lc,
+        w_res,
+        out_gain.reshape(1, width),
+        cotangent,
+    )
+    row_grads = row_grads.reshape(D, T, width)
+    new_moment1 = 0.9 * moment1 + 0.1 * row_grads
+    new_moment2 = 0.99 * moment2 + 0.01 * jnp.mean(row_grads * row_grads, -1)
+    row_step = new_moment1 * lax.rsqrt(new_moment2)[..., None]
+    return (layer_out, new_moment1, new_moment2, row_step)
+
+
+def step(C, R, *args):
+    if args[0].shape[1] == 8 and C == 16:
+        return fast_body(C, R, *args)
+    return plain_body(*args)
+
+
 def solution(mesh):
     return jax.shard_map(
-        body,
+        functools.partial(step, mesh.shape["col"], mesh.shape["row"]),
         mesh=mesh,
         in_specs=(
             P("row", "col", None),

time: 206 us -> 67.2 us (0.33)
  Pallas kernels: 0 us -> 57.4 us
  waiting for transfers between devices: 47.1 us -> 0 us
  local copies, waits for them, and re-layouts: 51.8 us -> 5.33 us
  matrix products: 30.7 us -> 0 us
  blocking collectives: 23.3 us -> 0 us
  starting transfers between devices: 17.1 us -> 0 us
  other arithmetic: 19.3 us -> 3.39 us
  between operations: 14.4 us -> 0.69 us
    pallas_call x0 -> x1, Pallas kernels: none -> 57.4 us  [fast_body(): pl.pallas_call(functools.partial(fused_kernel, C, R, D), out_shape=(jax.S...]
    all_to_all x4 -> x0, waiting for transfers between devices: 31.5 us -> none  [the longest x1 12.1 us: body(): lax.all_to_all(list_grads.reshape(columns, slot_dev, uniq * width), 'col'...]
    dot_general x14 -> x0, matrix products: 30.7 us -> none  [the longest x1 4 us: body(): lax.dot_general(part_rows, w_up, (((1,), (1,)), ((), ())), preferred_elem...]
    all_to_all x4 -> x0, starting transfers between devices: 17 us -> none  [the longest x1 5.83 us: body(): lax.all_to_all(list_grads.reshape(columns, slot_dev, uniq * width), 'col'...]
    reshape x14 -> x0, local copies, waits for them, and re-layouts: 16.9 us -> none  [the longest x1 2.67 us: body(): bucket.reshape(owners, capacity, width)]
    reduce_scatter x2 -> x0, waiting for transfers between devices: 15.5 us -> none  [the longest x1 8 us: body(): lax.psum_scatter(jnp.dot(part_rows, w_down, preferred_element_type=jnp.fl...]
    all_to_all x1 -> x0, blocking collectives: 13.6 us -> none  [body(): lax.all_to_all(index_local, 'col', split_axis=0, concat_axis=2, tiled=True)]
    scatter x2 -> x0, local copies, waits for them, and re-layouts: 10.7 us -> none  [the longest x1 6.37 us: body(): jnp.zeros((owners * capacity, width), jnp.float32).at[target_slot]]
  transfers between devices with their start and end apart: 6 -> 0, of which waited for: 5 -> 0; matrix products, arithmetic and copies ran while one was open for 14% -> 0% of each run, Pallas kernels for 0% -> 0%
where the time goes in v1:
time: 67.2 us; the launch traced here: 66.9 us
  Pallas kernels  57.4 us (85%)
  local copies, waits for them, and re-layouts  5.33 us (8%)
  other arithmetic  3.39 us (5%)
  between operations  0.69 us (1%)
    pallas_call x1, Pallas kernels, fast_body(): pl.pallas_call(functools.partial(fused_kernel, C, R, D), out_shape=(jax.S...  57.4 us
    unnamed x10, local copies, waits for them, and re-layouts  5.01 us
    mul x1, other arithmetic, fast_body(): new_moment1 = 0.9 * moment1 + 0.1 * row_grads  1.51 us

profile of v1, /device:TPU:0, one launch (start us, length us, event | category | flops | bytes accessed | tf_op | source)
XLA Modules:
  0.0 66.9 jit_solution(511494497472670163)
XLA Ops:
  0.6 1.4 %copy.19.fmp = bf16[128,8]{1,0:T(8,128)(2,1)} copy(bf16[128,8]{0,1:T(8,128)(2,1)} %param.16) | data formatting | bytes 4096 | tf_op args[3]
  2.0 1.5 %copy.18.rid = s32[16,8,8]{2,1,0:T(8,128)} copy(s32[16,8,8]{0,2,1:T(8,128)} %param.14) | data formatting | bytes 8192 | tf_op args[1]
  3.5 1.5 %copy.17 = s32[256,8]{1,0:T(8,128)} copy(s32[256,8]{0,1:T(8,128)} %param.15) | data formatting | bytes 16384 | tf_op args[2]
  5.0 57.4 %wukong_step.1 = (bf16[16,3072]{1,0:T(8,128)(2,1)}, f32[1024,192]{1,0:T(8,128)}) custom-call(bf16[16,8,1536]{2,1,0:T(8,128)(2,1)} %uniq.1, s32[16,8,8]{2,1,0:T(8,128)} %copy.18.rid, s32[16,16,8]{2,1,0:T(8,128)} %bitcast.8, bf16[128,8]{1,0:T(8,128)(2,1)} %copy.19.fmp, f32[1,1024]{1,0:T(1,128)} %bitcast.9, bf16[1024,1024]{1,0:T(8,128)(2,1)} %wup.1, ...), custom_call_target="tpu_custom_call" | custom-call | tf_op jit(solution)/shard_map/wukong_step/pallas_call | solution.py:591
  62.4 0.0 copy-start.2
  62.5 0.0 copy-start
  62.5 0.0 copy-start.1
  62.5 1.5 %broadcast_multiply_fusion = (f32[1024,192]{1,0:T(8,128)S(1)}, f32[1024]{0:T(1024)S(1)}) fusion(f32[1024,192]{1,0:T(8,128)} %get-tuple-element.7), kind=kLoop, calls=%fused_computation.2 | loop fusion | flops 588800 | bytes 1576960 | tf_op jit(solution)/shard_map/mul | solution.py:667
  64.0 0.3 copy.20
  64.3 0.0 copy-done.2
  64.3 0.6 fusion
  64.9 0.0 copy-done
  64.9 1.3 %broadcast_multiply_fusion.1 = (f32[8,128,192]{1,2,0:T(8,128)}, f32[8,128,192]{1,2,0:T(8,128)}) fusion(f32[8,128]{1,0:T(8,128)S(1)} %get-tuple-element.10, f32[8,128,192]{1,2,0:T(8,128)S(1)} %copy.20, f32[8,128,192]{1,2,0:T(8,128)S(1)} %copy-done), kind=kLoop, calls=%fused_computation.3 | loop fusion | flops 589824 | bytes 3149824 | tf_op jit(solution)/shard_map/mul | solution.py:669
  66.2 0.0 copy-done.1
  66.2 0.6 copy.22
Async XLA Ops:
  62.4 1.9 %copy-start.2 = (f32[8,128]{1,0:T(8,128)S(1)}, f32[8,128]{1,0:T(8,128)}, u32[]{:S(2)}) copy-start(f32[8,128]{1,0:T(8,128)} %param.25) | copy-start | bytes 12292
  62.5 2.5 %copy-start = (f32[8,128,192]{1,2,0:T(8,128)S(1)}, f32[8,128,192]{1,2,0:T(8,128)}, u32[]{:S(2)}) copy-start(f32[8,128,192]{1,2,0:T(8,128)} %param.24) | copy-start | bytes 2359300
  62.5 3.8 %copy-start.1 = (bf16[16,3072]{1,0:T(8,128)(2,1)S(1)}, bf16[16,3072]{1,0:T(8,128)(2,1)}, u32[]{:S(2)}) copy-start(bf16[16,3072]{1,0:T(8,128)(2,1)} %get-tuple-element.18) | copy-start | bytes 294916

commit v2 on v1

--- a/solution.py
+++ b/solution.py
@@ -198,6 +198,7 @@
     cot,
     lay_out,
     rg_out,
+    isend,
     land,
     iland,
     wraw,
@@ -211,6 +212,7 @@
     rmat,
     nrm,
     ggr,
+    idxn,
     nall,
     y,
     ds,
@@ -228,13 +230,8 @@
     sb,
     rland,
     oh,
-    enta,
-    entb,
-    owna,
-    psa,
-    pra,
-    psb,
-    prb,
+    ps,
+    pr,
     loc,
     s1,
     r1,
@@ -244,11 +241,12 @@
     ra,
     sbs,
     rbs,
+    sc,
+    rc,
     sx,
     rx,
 ):
     S, E, U, K, T = 16, 192, 8, 8, 128
-    DV = D * T
     me = lax.axis_index("col")
     mr = lax.axis_index("row")
 
@@ -277,11 +275,9 @@
     cp_up = pltpu.make_async_copy(wup, wraw, loc.at[0])
     cp_dn = pltpu.make_async_copy(wdn, wd, loc.at[1])
     own_rows = pltpu.make_async_copy(uniq.at[me], land.at[me], loc.at[2])
-    own_idx = pltpu.make_async_copy(sidx.at[me], iland.at[me], loc.at[3])
     cp_up.start()
     cp_dn.start()
     own_rows.start()
-    own_idx.start()
 
     barrier = pltpu.get_barrier_semaphore()
     for i in range(1, C):
@@ -292,22 +288,28 @@
         pl.semaphore_signal(
             barrier, inc=1, device_id={"row": to_row(i)}, device_id_type=pl.DeviceIdType.MESH
         )
+    for p in range(C):
+        at = p * S % T
+        tile = sidx[:, p * S // T * T : (p * S // T + 1) * T]
+        if at:
+            tile = pltpu.roll(tile, T - at, 1)
+        isend[p] = tile[:, :S]
+    iland[me] = isend[me]
     pl.semaphore_wait(barrier, C + R - 2)
 
     order = sorted(range(1, C), key=lambda i: -min(i, C - i))
     idx_copies, row_copies = [], []
     for i in order:
         p = to_col(i)
-        idx_copies.append(rcopy(sidx.at[p], iland.at[me], si.at[i], ri.at[i], {"col": p}))
+        idx_copies.append(rcopy(isend.at[p], iland.at[me], si.at[i], ri.at[i], {"col": p}))
         idx_copies[-1].start()
     for i in order:
         p = to_col(i)
         row_copies.append(rcopy(uniq.at[p], land.at[me], s1.at[i], r1.at[i], {"col": p}))
         row_copies[-1].start()
 
-    eye8 = (iota((K, K), 0) == iota((K, K), 1)).astype(F32)
-    pr, pc = iota((256, 256), 0), iota((256, 256), 1)
-    perm = (((pr & 31) * 8 + (pr >> 5)) == pc).astype(F32).astype(BF16)
+    to, at = iota((256, 256), 0), iota((256, 256), 1)
+    perm = (((to & 31) * 8 + (to >> 5)) == at).astype(F32).astype(BF16)
     cp_up.wait()
     for g in range(4):
         blk = matmul(perm, wraw[g * 256 : (g + 1) * 256, :]).astype(BF16)
@@ -320,7 +322,7 @@
 
     amat = jnp.concatenate(
         [
-            matmul(eye8.astype(BF16), fmp[...], NT),
+            fmp[...].astype(F32),
             wlc[...].astype(F32),
             wres[...].astype(F32),
         ],
@@ -329,40 +331,47 @@
     for j in range(32):
         arep[j * S : (j + 1) * S, :] = jnp.broadcast_to(amat[j : j + 1, :], (S, T))
 
-    labels = matmul(eye8, rid[...].astype(F32).reshape(C * D, U), NT, HIGH).astype(jnp.int32)
-    slot_lane = iota((U, T), 1) & (D - 1)
-    target = iota((DV, T), 0)
+    place = (iota((C, T), 0) == (iota((C, T), 1) >> 3)).astype(F32)
+    wide = matmul(rid[...].astype(F32).reshape(D * U, C), place, precision=HIGH).reshape(D, U, T)
+    mine = iota((D, U, T), 1) == (iota((D, U, T), 2) & (U - 1))
+    labels = jnp.sum(jnp.where(mine, wide, 0.0), 1).astype(jnp.int32)
+    target = iota((T, T), 0)
     for i in range(R):
         local = labels - to_row(i) * T
-        key = jnp.where((local >= 0) & (local < T), slot_lane * T + local, -1)
-        for u in range(U):
-            oh[i, :, u * T : (u + 1) * T] = jnp.where(
-                target == jnp.broadcast_to(key[u : u + 1, :], (DV, T)), 1.0, 0.0
+        for d in range(D):
+            oh[i, d] = jnp.where(
+                target == jnp.broadcast_to(local[d : d + 1, :], (T, T)), 1.0, 0.0
             ).astype(BF16)
 
-    own_idx.wait()
     for cp in idx_copies:
         cp.wait_recv()
-    ix = iland[...].astype(F32).reshape(C * S, D)
-    tl = iota((C * S, T), 1)
-    placed = jnp.zeros((C * S, T), F32)
-    for d in range(D):
-        placed = jnp.where((tl & (D - 1)) == d, ix[:, d : d + 1], placed)
-    placed = jnp.where((tl >> (D.bit_length() - 1)) == (iota((C * S, T), 0) >> 4), placed, 0.0)
-    ist = jnp.sum(placed.reshape(C, S, T), 0)
-    idx_t = jnp.concatenate([ist] * 8, 0)
-    idx_n = idx_t.T
+    ix = iland[...].astype(F32).reshape(T, S)
+    tiled = (iota((S, T), 0) == (iota((S, T), 1) & (S - 1))).astype(F32)
+    idx_n = matmul(ix, tiled, precision=HIGH)
+    idxn[...] = idx_n
+    idx_t = idx_n.T
     for u in range(U):
         for q in range(4):
             lm[q * T : (q + 1) * T, u * T : (u + 1) * T] = jnp.where(
                 idx_t == float(u), arep[q * T : (q + 1) * T, :], 0.0
             ).astype(BF16)
+    entry = iota((U, T), 0).astype(F32)
+
+    def fill(src, q):
+        for t in range(0, T, 2):
+            rows = [
+                jnp.where(
+                    jnp.broadcast_to(idxn[v : v + 1, :], (U, T)) == entry,
+                    jnp.broadcast_to(src[v : v + 1, :], (U, T)),
+                    0.0,
+                )
+                for v in (t, t + 1)
+            ]
+            lmask[t * U : (t + 2) * U, q * T : (q + 1) * T] = jnp.concatenate(rows, 0).astype(BF16)
+
     for q in range(4):
-        turned = arep[q * T : (q + 1) * T, :].T
-        for u in range(U):
-            lmask[u * T : (u + 1) * T, q * T : (q + 1) * T] = jnp.where(
-                idx_n == float(u), turned, 0.0
-            ).astype(BF16)
+        ggr[...] = arep[q * T : (q + 1) * T, :].T
+        fill(ggr, q)
     upstream = cot[...].astype(F32)
     for o in range(16):
         rmat[(16 + o) * S : (17 + o) * S, :] = upstream[:, o * E : (o + 1) * E].astype(BF16)
@@ -460,90 +469,70 @@
     for k in range(K):
         ggr[k * S : (k + 1) * S, :] = (qs[k] - first - ns[k] * second) * inv_in
     gg = ggr[...]
-    ggt = gg.T
     for u in range(U):
         lm[0:T, u * T : (u + 1) * T] = jnp.where(idx_t == float(u), gg, 0.0).astype(BF16)
-        lmask[u * T : (u + 1) * T, 512:640] = jnp.where(idx_n == float(u), ggt, 0.0).astype(BF16)
+    ggr[...] = gg.T
+    fill(ggr, 4)
     rmat[0:T, :] = matmul(lm[0:T, :], tst[...]).astype(BF16)
     lg[...] = matmul(lmask[...], rmat[...])
 
-    half = iota((T, T), 1) < 64
-
-    def lo(u):
-        return lg[u * T : (u + 1) * T, 0:T].reshape(C, D, T)
-
-    def hi(u):
-        a = lg[u * T : (u + 1) * T, T:E]
-        b = lg[(u + 4) * T : (u + 5) * T, T:E]
-        return jnp.concatenate([a, b], 1).reshape(C, D, T)
-
-    for p in range(2):
-        sb[:, 64 + p * 16 : 80 + p * 16, :] = jnp.concatenate([hi(2 * p), hi(2 * p + 1)], 1).astype(
-            BF16
-        )
-    for p in range(4):
-        sb[:, p * 16 : (p + 1) * 16, :] = jnp.concatenate([lo(2 * p), lo(2 * p + 1)], 1).astype(
-            BF16
-        )
-    cut_a, cut_b = pl.ds(0, 64), pl.ds(64, 32)
-    b_copies, a_copies = [], []
-    for i in order:
-        p = to_col(i)
-        b_copies.append(
-            rcopy(sb.at[p, cut_b], rland.at[me, cut_b], sbs.at[i], rbs.at[i], {"col": p})
-        )
-        b_copies[-1].start()
-    for i in order:
-        p = to_col(i)
-        a_copies.append(rcopy(sb.at[p, cut_a], rland.at[me, cut_a], sa.at[i], ra.at[i], {"col": p}))
-        a_copies[-1].start()
+    top = lg[:, T:E].reshape(C, D * U, E - T)
+    sb[:, 64:96, :] = jnp.concatenate([top[:, :32], top[:, 32:]], -1).astype(BF16)
+    sb[:, 0:64, :] = lg[:, 0:T].reshape(C, D * U, T).astype(BF16)
+    cuts = (pl.ds(64, 32), pl.ds(0, 32), pl.ds(32, 32))
+    sems = ((sbs, rbs), (sa, ra), (sc, rc))
+    g_in = []
+    for cut, (ssem, rsem) in zip(cuts, sems):
+        g_in.append([])
+        for i in order:
+            p = to_col(i)
+            g_in[-1].append(
+                rcopy(sb.at[p, cut], rland.at[me, cut], ssem.at[i], rsem.at[i], {"col": p})
+            )
+            g_in[-1][-1].start()
     rland[me] = sb[me]
 
-    for cp in b_copies:
-        cp.wait_recv()
-    for p in range(2):
-        both = rland[:, 64 + p * 16 : 80 + p * 16, :].astype(F32)
-        for h in range(2):
-            u = 2 * p + h
-            x = both[:, h * D : (h + 1) * D, :].reshape(T, T)
-            entb[u * T : (u + 1) * T, :] = x.astype(BF16)
-            entb[(u + 4) * T : (u + 5) * T, :] = pltpu.roll(x, 64, 1).astype(BF16)
-    hd = DV // 2
-    low = iota((hd, T), 1) < 64
     p_copies = []
-    for i in range(1, R):
-        full = matmul(oh[i], entb[...])
-        psb[i] = jnp.where(low, full[:hd], pltpu.roll(full[hd:], 64, 1)).astype(BF16)
-        p_copies.append(
-            rcopy(psb.at[i], prb.at[i], sx.at[4 * R + i], rx.at[4 * R + i], {"row": to_row(i)})
-        )
-        p_copies[-1].start()
-    rg_out[:, T:E] = matmul(oh[0], entb[...])[:, : E - T]
-
-    for cp in a_copies:
-        cp.wait_recv()
-    for p in range(4):
-        both = rland[:, p * 16 : (p + 1) * 16, :].astype(F32)
-        for h in range(2):
-            u = 2 * p + h
-            enta[u * T : (u + 1) * T, :] = both[:, h * D : (h + 1) * D, :].reshape(T, T).astype(BF16)
-    for i in range(1, R):
-        psa[i] = matmul(oh[i], enta[...]).astype(BF16)
-        p_copies.append(
-            rcopy(psa.at[i], pra.at[i], sx.at[5 * R + i], rx.at[5 * R + i], {"row": to_row(i)})
-        )
-        p_copies[-1].start()
-    owna[...] = matmul(oh[0], enta[...])
+    for stage in range(3):
+        for cp in g_in[stage]:
+            cp.wait_recv()
+        pieces = []
+        for p in range(2):
+            start = (64, 0, 32)[stage] + p * 16
+            both = rland[:, start : start + 16, :].astype(F32)
+            for h in range(2):
+                x = both[:, h * U : (h + 1) * U, :].reshape(T, T).T.astype(BF16)
+                d = 2 * p + h
+                if stage == 0:
+                    pieces.append((d, T, E, x[: E - T]))
+                    pieces.append((d + 4, T, E, x[E - T :]))
+                else:
+                    pieces.append((d + 4 * (stage - 1), 0, T, x))
+        for i in range(1, R):
+            for d, a, b, x in pieces:
+                ps[i, d, a:b, :] = matmul(x, oh[i, d], NT).astype(BF16)
+            part = (slice(0, D), slice(T, E)) if stage == 0 else (
+                slice(4 * (stage - 1), 4 * stage),
+                slice(0, T),
+            )
+            ds_of = tuple(pl.ds(q.start, q.stop - q.start) for q in part)
+            sem = (4 + stage) * R + i
+            p_copies.append(
+                rcopy(
+                    ps.at[(i,) + ds_of],
+                    pr.at[(i,) + ds_of],
+                    sx.at[sem],
+                    rx.at[sem],
+                    {"row": to_row(i)},
+                )
+            )
+            p_copies[-1].start()
+        for d, a, b, x in pieces:
+            rg_out[d, a:b, :] = matmul(x, oh[0, d], NT)
     for cp in p_copies:
         cp.wait_recv()
-    total = owna[...]
     for i in range(1, R):
-        total = total + pra[i].astype(F32)
-    rg_out[:, 0:T] = total
-    for i in range(1, R):
-        x = prb[i].astype(F32)
-        rg_out[:hd, T:E] += x[:, : E - T]
-        rg_out[hd:, T:E] += pltpu.roll(x, 64, 1)[:, : E - T]
+        rg_out[...] += pr[i].astype(F32)
 
     for group in (
         idx_copies,
@@ -552,12 +541,25 @@
         f_copies,
         g_copies,
         q_copies,
-        b_copies,
-        a_copies,
+        g_in[0],
+        g_in[1],
+        g_in[2],
         p_copies,
     ):
         for cp in group:
             cp.wait_send()
+
+
+def moment_kernel(width, lay, grads, m1, m2, lay_out, m1_out, m2_out, step_out):
+    lay_out[...] = lay[...]
+    for h in range(2):
+        row = pl.ds(pl.program_id(0) * 2 + h, 1)
+        g = grads[h]
+        first = 0.9 * m1[h] + 0.1 * g
+        second = 0.99 * m2[row, :] + 0.01 * (jnp.sum(g * g, 0, keepdims=True) / width)
+        m1_out[h] = first
+        m2_out[row, :] = second
+        step_out[h] = first * lax.rsqrt(second)
 
 
 def fast_body(
@@ -584,7 +586,6 @@
     flat = w_up.shape[0]
     width = out_gain.shape[0]
     T = C * D
-    DV = D * T
     vmem = pl.BlockSpec(memory_space=pltpu.VMEM)
     hbm = pl.BlockSpec(memory_space=pl.ANY)
     dma = pltpu.SemaphoreType.DMA
@@ -592,13 +593,14 @@
         functools.partial(fused_kernel, C, R, D),
         out_shape=(
             jax.ShapeDtypeStruct((S, 16 * width), BF16),
-            jax.ShapeDtypeStruct((DV, width), F32),
+            jax.ShapeDtypeStruct((D, width, T), F32),
         ),
-        in_specs=[hbm, vmem, hbm, vmem, vmem, hbm, hbm, vmem, vmem, vmem, vmem],
+        in_specs=[hbm, vmem, vmem, vmem, vmem, hbm, hbm, vmem, vmem, vmem, vmem],
         out_specs=(vmem, vmem),
         scratch_shapes=[
+            pltpu.VMEM((C, D, S), jnp.int32),
             pltpu.VMEM((C, D, wide), BF16),
-            pltpu.VMEM((C, S, D), jnp.int32),
+            pltpu.VMEM((C, D, S), jnp.int32),
             pltpu.VMEM((flat, hid), BF16),
             pltpu.VMEM((flat, hid), BF16),
             pltpu.VMEM((hid, wide), BF16),
@@ -610,6 +612,7 @@
             pltpu.VMEM((640, width), BF16),
             pltpu.VMEM((128, T), F32),
             pltpu.VMEM((128, T), F32),
+            pltpu.VMEM((T, 128), F32),
             pltpu.VMEM((R, S, flat), BF16),
             pltpu.VMEM((384, width), F32),
             pltpu.VMEM((R * S, hid), F32),
@@ -626,14 +629,9 @@
             pltpu.VMEM((8 * T, width), F32),
             pltpu.VMEM((C, 12 * D, T), BF16),
             pltpu.VMEM((C, 12 * D, T), BF16),
-            pltpu.VMEM((R, DV, 8 * T), BF16),
-            pltpu.VMEM((8 * T, T), BF16),
-            pltpu.VMEM((8 * T, T), BF16),
-            pltpu.VMEM((DV, T), F32),
-            pltpu.VMEM((R, DV, T), BF16),
-            pltpu.VMEM((R, DV, T), BF16),
-            pltpu.VMEM((R, DV // 2, T), BF16),
-            pltpu.VMEM((R, DV // 2, T), BF16),
+            pltpu.VMEM((R, D, T, T), BF16),
+            pltpu.VMEM((R, D, width, T), BF16),
+            pltpu.VMEM((R, D, width, T), BF16),
             dma((4,)),
             dma((C,)),
             dma((C,)),
@@ -643,8 +641,10 @@
             dma((C,)),
             dma((C,)),
             dma((C,)),
-            dma((6 * R,)),
-            dma((6 * R,)),
+            dma((C,)),
+            dma((C,)),
+            dma((7 * R,)),
+            dma((7 * R,)),
         ],
         compiler_params=pltpu.CompilerParams(
             collective_id=0, has_side_effects=True, vmem_limit_bytes=56 * 1024 * 1024
@@ -652,9 +652,9 @@
         name="wukong_step",
     )(
         uniq_rows,
-        row_ids,
-        sample_idx.reshape(C, S, D),
-        fm_proj,
+        row_ids.transpose(1, 2, 0),
+        sample_idx.T,
+        fm_proj.T,
         ln_gain.reshape(1, flat),
         w_up,
         w_down,
@@ -663,11 +663,28 @@
         out_gain.reshape(1, width),
         cotangent,
     )
-    row_grads = row_grads.reshape(D, T, width)
-    new_moment1 = 0.9 * moment1 + 0.1 * row_grads
-    new_moment2 = 0.99 * moment2 + 0.01 * jnp.mean(row_grads * row_grads, -1)
-    row_step = new_moment1 * lax.rsqrt(new_moment2)[..., None]
-    return (layer_out, new_moment1, new_moment2, row_step)
+    slab = pl.BlockSpec((2, width, T), lambda d: (d, 0, 0))
+    whole = pl.BlockSpec((D, T), lambda d: (0, 0))
+    strip = pl.BlockSpec((S, 8 * width // (D // 4)), lambda d: (0, d))
+    layer_out, new_moment1, new_moment2, row_step = pl.pallas_call(
+        functools.partial(moment_kernel, width),
+        grid=(D // 2,),
+        out_shape=(
+            jax.ShapeDtypeStruct((S, 16 * width), BF16),
+            jax.ShapeDtypeStruct((D, width, T), F32),
+            jax.ShapeDtypeStruct((D, T), F32),
+            jax.ShapeDtypeStruct((D, width, T), F32),
+        ),
+        in_specs=[strip, slab, slab, whole],
+        out_specs=(strip, slab, whole, slab),
+        name="moments",
+    )(layer_out, row_grads, moment1.transpose(0, 2, 1), moment2)
+    return (
+        layer_out,
+        new_moment1.transpose(0, 2, 1),
+        new_moment2,
+        row_step.transpose(0, 2, 1),
+    )
 
 
 def step(C, R, *args):

time: 67.2 us -> 59.7 us (0.89)
  local copies, waits for them, and re-layouts: 5.33 us -> 0 us
  other arithmetic: 3.39 us -> 0 us
  Pallas kernels: 57.4 us -> 58.9 us
    unnamed x10 -> x0, local copies, waits for them, and re-layouts: 5.01 us -> none
    pallas_call x0 -> x1, Pallas kernels: none -> 3.69 us  [fast_body(): pl.pallas_call(functools.partial(moment_kernel, width), grid=(D // 2,), o...]
    mul x2 -> x0, other arithmetic: 2.8 us -> none  [the longest x1 1.51 us: fast_body(): new_moment1 = 0.9 * moment1 + 0.1 * row_grads]
    pallas_call x1, Pallas kernels: 57.4 us -> 55.2 us  [fast_body(): pl.pallas_call(functools.partial(fused_kernel, C, R, D), out_shape=(jax.S...]
where the time goes in v2:
time: 59.7 us; the launch traced here: 59.5 us
  Pallas kernels  58.9 us (99%)
  between operations  0.64 us (1%)
    pallas_call x1, Pallas kernels, fast_body(): pl.pallas_call(functools.partial(fused_kernel, C, R, D), out_shape=(jax.S...  55.2 us
    pallas_call x1, Pallas kernels, fast_body(): pl.pallas_call(functools.partial(moment_kernel, width), grid=(D // 2,), o...  3.69 us

profile of v2, /device:TPU:0, one launch (start us, length us, event | category | flops | bytes accessed | tf_op | source)
XLA Modules:
  0.0 59.5 jit_solution(7640919566324786770)
XLA Ops:
  0.6 55.2 %wukong_step.1 = (bf16[16,3072]{1,0:T(8,128)(2,1)}, f32[8,192,128]{2,1,0:T(8,128)}) custom-call(bf16[16,8,1536]{2,1,0:T(8,128)(2,1)} %uniq.1, s32[8,8,16]{2,1,0:T(8,128)} %bitcast.9, s32[8,256]{1,0:T(8,128)} %bitcast.10, bf16[8,128]{1,0:T(8,128)(2,1)} %bitcast.12, f32[1,1024]{1,0:T(1,128)} %bitcast.11, bf16[1024,1024]{1,0:T(8,128)(2,1)} %wup.1, ...), custom_call_target="tpu_custom_call" | custom-call | tf_op jit(solution)/shard_map/wukong_step/pallas_call | solution.py:592
  55.8 3.7 %moments.1 = (bf16[16,3072]{1,0:T(8,128)(2,1)}, f32[8,192,128]{2,1,0:T(8,128)}, f32[8,128]{1,0:T(8,128)}, f32[8,192,128]{2,1,0:T(8,128)}) custom-call(bf16[16,3072]{1,0:T(8,128)(2,1)} %get-tuple-element.10.lay, f32[8,192,128]{2,1,0:T(8,128)} %get-tuple-element.11.grads, f32[8,192,128]{2,1,0:T(8,128)} %bitcast.8, f32[8,128]{1,0:T(8,128)} %m2.1), custom_call_target="tpu_custom_call" | custom-call | tf_op jit(solution)/shard_map/moments/pallas_call | solution.py:669

commit v3 on v2

--- a/solution.py
+++ b/solution.py
@@ -275,8 +275,6 @@
     cp_up = pltpu.make_async_copy(wup, wraw, loc.at[0])
     cp_dn = pltpu.make_async_copy(wdn, wd, loc.at[1])
     own_rows = pltpu.make_async_copy(uniq.at[me], land.at[me], loc.at[2])
-    cp_up.start()
-    cp_dn.start()
     own_rows.start()
 
     barrier = pltpu.get_barrier_semaphore()
@@ -308,6 +306,9 @@
         row_copies.append(rcopy(uniq.at[p], land.at[me], s1.at[i], r1.at[i], {"col": p}))
         row_copies[-1].start()
 
+    cp_up.start()
+    cp_dn.start()
+
     to, at = iota((256, 256), 0), iota((256, 256), 1)
     perm = (((to & 31) * 8 + (to >> 5)) == at).astype(F32).astype(BF16)
     cp_up.wait()
@@ -423,6 +424,8 @@
     ds[...] = sg * (1.0 + hp * (1.0 - sg))
 
     gain_out = og[...]
+    up_fm = jnp.concatenate([upstream[:, o * E : (o + 1) * E] for o in range(8)], 0) * gain_out
+    up_mean = jnp.mean(up_fm, -1, keepdims=True)
 
     def out_norm(joined, o):
         up = upstream[:, o * E : (o + 1) * E]
@@ -442,12 +445,20 @@
     for i in range(1, R):
         total = total + frecv[from_row(i)].astype(F32)
     fm[...] = total
+    joined = jnp.concatenate([fm[:, o * E : (o + 1) * E] for o in range(8)], 0)
+    cen = joined - jnp.mean(joined, -1, keepdims=True)
+    inv_fm = lax.rsqrt(jnp.mean(cen * cen, -1, keepdims=True) + 1e-05)
+    normed_fm = cen * inv_fm
+    across = jnp.mean(up_fm * cen, -1, keepdims=True) * inv_fm
+    grad_fm = (up_fm - up_mean - normed_fm * across) * inv_fm
     for o in range(8):
-        nr, gj = out_norm(fm[:, o * E : (o + 1) * E], o)
-        lay32[:, o * E : (o + 1) * E] = nr * gain_out + y[(8 + o) * S : (9 + o) * S, :]
-        gf32[:, o * E : (o + 1) * E] = gj
+        gf32[:, o * E : (o + 1) * E] = grad_fm[o * S : (o + 1) * S]
     gall[mr] = gf32[...].astype(BF16)
     g_copies = row_send(2, lambda p: gall.at[mr], gall)
+    for o in range(8):
+        lay32[:, o * E : (o + 1) * E] = (
+            normed_fm[o * S : (o + 1) * S] * gain_out + y[(8 + o) * S : (9 + o) * S, :]
+        )
     lay_out[...] = lay32[...].astype(BF16)
     for cp in g_copies:
         cp.wait_recv()
@@ -482,14 +493,19 @@
     cuts = (pl.ds(64, 32), pl.ds(0, 32), pl.ds(32, 32))
     sems = ((sbs, rbs), (sa, ra), (sc, rc))
     g_in = []
-    for cut, (ssem, rsem) in zip(cuts, sems):
+
+    def send_lists(stage):
+        cut, (ssem, rsem) = cuts[stage], sems[stage]
         g_in.append([])
         for i in order:
             p = to_col(i)
-            g_in[-1].append(
+            g_in[stage].append(
                 rcopy(sb.at[p, cut], rland.at[me, cut], ssem.at[i], rsem.at[i], {"col": p})
             )
-            g_in[-1][-1].start()
+            g_in[stage][-1].start()
+
+    send_lists(0)
+    send_lists(1)
     rland[me] = sb[me]
 
     p_copies = []
@@ -527,6 +543,8 @@
                 )
             )
             p_copies[-1].start()
+        if stage == 0:
+            send_lists(2)
         for d, a, b, x in pieces:
             rg_out[d, a:b, :] = matmul(x, oh[0, d], NT)
     for cp in p_copies:
@@ -552,8 +570,8 @@
 
 def moment_kernel(width, lay, grads, m1, m2, lay_out, m1_out, m2_out, step_out):
     lay_out[...] = lay[...]
-    for h in range(2):
-        row = pl.ds(pl.program_id(0) * 2 + h, 1)
+    for h in range(4):
+        row = pl.ds(pl.program_id(0) * 4 + h, 1)
         g = grads[h]
         first = 0.9 * m1[h] + 0.1 * g
         second = 0.99 * m2[row, :] + 0.01 * (jnp.sum(g * g, 0, keepdims=True) / width)
@@ -663,12 +681,12 @@
         out_gain.reshape(1, width),
         cotangent,
     )
-    slab = pl.BlockSpec((2, width, T), lambda d: (d, 0, 0))
+    slab = pl.BlockSpec((4, width, T), lambda d: (d, 0, 0))
     whole = pl.BlockSpec((D, T), lambda d: (0, 0))
-    strip = pl.BlockSpec((S, 8 * width // (D // 4)), lambda d: (0, d))
+    strip = pl.BlockSpec((S, 8 * width), lambda d: (0, d))
     layer_out, new_moment1, new_moment2, row_step = pl.pallas_call(
         functools.partial(moment_kernel, width),
-        grid=(D // 2,),
+        grid=(D // 4,),
         out_shape=(
             jax.ShapeDtypeStruct((S, 16 * width), BF16),
             jax.ShapeDtypeStruct((D, width, T), F32),

time: 59.7 us -> 57.7 us (0.966)
  Pallas kernels: 58.9 us -> 56.8 us
    pallas_call x1, Pallas kernels: 3.69 us -> 2.39 us  [fast_body(): pl.pallas_call(functools.partial(moment_kernel, width), grid=(D // 4,), o...]
    pallas_call x1, Pallas kernels: 55.2 us -> 54.4 us  [fast_body(): pl.pallas_call(functools.partial(fused_kernel, C, R, D), out_shape=(jax.S...]
where the time goes in v3:
time: 57.7 us; the launch traced here: 57.5 us
  Pallas kernels  56.8 us (98%)
  between operations  0.64 us (1%)
    pallas_call x1, Pallas kernels, fast_body(): pl.pallas_call(functools.partial(fused_kernel, C, R, D), out_shape=(jax.S...  54.4 us
    pallas_call x1, Pallas kernels, fast_body(): pl.pallas_call(functools.partial(moment_kernel, width), grid=(D // 4,), o...  2.39 us

profile of v3, /device:TPU:0, one launch (start us, length us, event | category | flops | bytes accessed | tf_op | source)
XLA Modules:
  0.0 57.5 jit_solution(2942115318562266016)
XLA Ops:
  0.6 54.4 %wukong_step.1 = (bf16[16,3072]{1,0:T(8,128)(2,1)}, f32[8,192,128]{2,1,0:T(8,128)}) custom-call(bf16[16,8,1536]{2,1,0:T(8,128)(2,1)} %uniq.1, s32[8,8,16]{2,1,0:T(8,128)} %bitcast.9, s32[8,256]{1,0:T(8,128)} %bitcast.10, bf16[8,128]{1,0:T(8,128)(2,1)} %bitcast.12, f32[1,1024]{1,0:T(1,128)} %bitcast.11, bf16[1024,1024]{1,0:T(8,128)(2,1)} %wup.1, ...), custom_call_target="tpu_custom_call" | custom-call | tf_op jit(solution)/shard_map/wukong_step/pallas_call | solution.py:610
  55.1 2.4 %moments.1 = (bf16[16,3072]{1,0:T(8,128)(2,1)}, f32[8,192,128]{2,1,0:T(8,128)}, f32[8,128]{1,0:T(8,128)}, f32[8,192,128]{2,1,0:T(8,128)}) custom-call(bf16[16,3072]{1,0:T(8,128)(2,1)} %get-tuple-element.10.lay, f32[8,192,128]{2,1,0:T(8,128)} %get-tuple-element.11.grads, f32[8,192,128]{2,1,0:T(8,128)} %bitcast.8, f32[8,128]{1,0:T(8,128)} %m2.1), custom_call_target="tpu_custom_call" | custom-call | tf_op jit(solution)/shard_map/moments/pallas_call | solution.py:687
